TPU v7x, 32 devices: a whole 2x2x4 slice. The times are simulated.
32 devices in a mesh: ctx: 8 (over y, x, core), head: 4 (over z).
Axes of the slice: x: 2, y: 2, z: 4, core: 2. Of those that a mesh axis runs over, the one named last changes fastest.
Arguments:
- head_inputs: bfloat16 [8192, 8192], P(('ctx', 'head')), may hold values from -6 to 6
- gate_inputs: bfloat16 [8192, 8192], P(('ctx', 'head')), may hold values from -6 to 6
- write_keys: bfloat16 [8192, 1024], P(('ctx', 'head')), may hold values from -6 to 6
- read_queries: bfloat16 [8192, 1024], P(('ctx', 'head')), may hold values from -0.5 to 0.5
- step_logits: bfloat16 [8192, 128], P(('ctx', 'head')), may hold values from -3 to 3
- step_bias: float32 [128], P('head'), may hold values from -6 to 0
- decay_log: float32 [128], P('head'), may hold values from -7 to -2
- skip_scale: float32 [128], P('head'), may hold values from 0.5 to 1.5
- norm_gain: float32 [8192], replicated, may hold values from 0.1 to 1.9
- document_starts: int32 [32], P('ctx'), may hold values from 0 to 256, as said below
Outputs:
- layer_output: bfloat16 [8192, 8192], P(('ctx', 'head'))
Inputs may be any that keep to these rules, and one draw needn't show every extreme that they name: `document_starts`: each entry is the position within its block of 256 tokens at which a document starts, or 256 where none starts; the first block starts one at 0.
All inputs are finite; a program needn't handle non-finite values.
Results may differ from a plain program's by a relative error of at most 0.0058.
Values may be sent and summed in bfloat16 or wider, within the bound.
A program may use at most 128 MiB of HBM per device.

v0:
```python
import jax
import jax.numpy as jnp
from jax import lax
from jax.sharding import PartitionSpec as P

HEAD_DIM = 64
STATE = 128
BLOCK = 256


def block_terms(block_x, block_b, block_c, block_logit, start_at, step_bias, decay_log):
    length = block_x.shape[0]
    per_group = block_x.shape[1] // block_b.shape[1]
    step_size = jax.nn.softplus(block_logit.astype(jnp.float32) + step_bias)
    log_decay = -jnp.exp(decay_log) * step_size
    cumulative = jnp.cumsum(log_decay, axis=0)
    position = jnp.arange(length, dtype=jnp.int32)
    segment = position >= start_at
    allowed = (segment[:, None] == segment[None, :]) & (position[:, None] >= position[None, :])
    scores = jnp.einsum("tgn,sgn->gts", block_c, block_b, preferred_element_type=jnp.float32)
    scores = jnp.repeat(scores, per_group, axis=0)
    across = cumulative.T
    spread = across[:, :, None] - across[:, None, :]
    damping = jnp.where(allowed[None], jnp.exp(jnp.where(allowed[None], spread, 0.0)), 0.0)
    mixing = (damping * scores * step_size.T[:, None, :]).astype(jnp.bfloat16)
    inside = jnp.einsum("hts,shp->thp", mixing, block_x, preferred_element_type=jnp.float32)
    keep = segment == segment[length - 1]
    tail = (
        jnp.where(keep[:, None], jnp.exp(cumulative[length - 1][None, :] - cumulative), 0.0)
        * step_size
    )
    scaled = (block_x.astype(jnp.float32) * tail[:, :, None]).astype(jnp.bfloat16)
    keys_heads = jnp.repeat(block_b, per_group, axis=1)
    written = jnp.einsum("thp,thn->hpn", scaled, keys_heads, preferred_element_type=jnp.float32)
    carried = jnp.where(start_at >= length, jnp.exp(cumulative[length - 1]), 0.0)
    return (inside, written, carried, cumulative, segment)


def local(
    head_inputs,
    gate_inputs,
    write_keys,
    read_queries,
    step_logits,
    step_bias,
    decay_log,
    skip_scale,
    norm_gain,
    document_starts,
):
    local_heads = step_bias.shape[0]
    head_x, head_b, head_c, head_logit = (
        lax.all_to_all(head_inputs, "head", split_axis=1, concat_axis=0, tiled=True),
        lax.all_to_all(write_keys, "head", split_axis=1, concat_axis=0, tiled=True),
        lax.all_to_all(read_queries, "head", split_axis=1, concat_axis=0, tiled=True),
        lax.all_to_all(step_logits, "head", split_axis=1, concat_axis=0, tiled=True),
    )
    length = head_x.shape[0]
    blocks = length // BLOCK
    group_count = head_b.shape[1] // STATE
    per_group = local_heads // group_count
    x_blocks = head_x.reshape(blocks, BLOCK, local_heads, HEAD_DIM)
    b_blocks = head_b.reshape(blocks, BLOCK, group_count, STATE)
    c_blocks = head_c.reshape(blocks, BLOCK, group_count, STATE)
    logit_blocks = head_logit.reshape(blocks, BLOCK, local_heads)

    def local_block(items):
        block_x, block_b, block_c, block_logit, start_at = items
        return block_terms(block_x, block_b, block_c, block_logit, start_at, step_bias, decay_log)

    inside, written, carried, cumulative, segment = lax.map(
        local_block, (x_blocks, b_blocks, c_blocks, logit_blocks, document_starts)
    )

    def summarize(carry_pair, items):
        total, running = carry_pair
        factor, term = items
        return ((total * factor, factor[:, None, None] * running + term), None)

    zero_state = jnp.zeros((local_heads, HEAD_DIM, STATE), jnp.float32)
    (own_decay, own_state), _ = lax.scan(
        summarize, (jnp.ones((local_heads,), jnp.float32), zero_state), (carried, written)
    )
    decays = lax.all_gather(own_decay[None], "ctx", axis=0, tiled=True)
    count = decays.shape[0]
    mine = lax.axis_index("ctx")
    order = jnp.arange(count, dtype=jnp.int32)
    between = (order[None, :] > order[:, None]) & (order[None, :] < mine)
    through = jnp.prod(jnp.where(between[:, :, None], decays[None, :, :], 1.0), axis=1)
    through = jnp.where((order < mine)[:, None], through, 0.0)
    incoming = jnp.sum(
        through[:, :, None, None] * lax.all_gather(own_state[None], "ctx", axis=0, tiled=True),
        axis=0,
    )

    def advance(running, items):
        block_x, block_c, inside_part, carried_part, written_part, cumulative_part, segment_part = (
            items
        )
        frozen = running.astype(jnp.bfloat16)
        query_heads = jnp.repeat(block_c, per_group, axis=1)
        outside = jnp.einsum(
            "thn,hpn->thp", query_heads, frozen, preferred_element_type=jnp.float32
        )
        factor = jnp.where(segment_part[:, None], 0.0, jnp.exp(cumulative_part))
        mixed = (
            inside_part
            + outside * factor[:, :, None]
            + skip_scale[None, :, None] * block_x.astype(jnp.float32)
        ).astype(jnp.bfloat16)
        return (carried_part[:, None, None] * running + written_part, mixed)

    _, mixed = lax.scan(
        advance, incoming, (x_blocks, c_blocks, inside, carried, written, cumulative, segment)
    )
    scanned = mixed.reshape(length, local_heads * HEAD_DIM)
    returned = lax.all_to_all(scanned, "head", split_axis=0, concat_axis=1, tiled=True)
    gated = returned.astype(jnp.float32) * jax.nn.silu(gate_inputs.astype(jnp.float32))
    power = jnp.mean(gated * gated, axis=-1, keepdims=True)
    return (gated * lax.rsqrt(power + 1e-05) * norm_gain).astype(jnp.bfloat16)


def solution(mesh):
    return jax.shard_map(
        local,
        mesh=mesh,
        in_specs=(
            P(("ctx", "head"), None),
            P(("ctx", "head"), None),
            P(("ctx", "head"), None),
            P(("ctx", "head"), None),
            P(("ctx", "head"), None),
            P("head"),
            P("head"),
            P("head"),
            P(),
            P("ctx"),
        ),
        out_specs=P(("ctx", "head"), None),
        check_vma=False,
    )
```

profile of v0, /device:TPU:0, one launch (start us, length us, event | category | flops | bytes accessed | tf_op | source)
XLA Modules:
  0.0 439.0 jit_solution(11517888740145431058)
XLA Ops:
  8.1 6.3 %all-to-all-start.1 = ((bf16[256,4,32]{0,2,1:T(8,128)(2,1)}), bf16[256,4,32]{0,2,1:T(8,128)(2,1)S(1)}, u32[]{:S(2)}, u32[]{:S(2)}) async-start(bf16[256,4,32]{0,2,1:T(8,128)(2,1)} %bitcast.29), calls=%async_computation.1 | async-start | bytes 131072 | tf_op jit(solution)/shard_map/all_to_all | solution.py:56
  16.5 3.7 all-to-all-done.1
  20.2 3.5 all-to-all-start.2
  25.7 11.3 %all-to-all-done.2 = bf16[256,4,256]{0,2,1:T(8,128)(2,1)S(1)} async-done(((bf16[256,4,256]{0,2,1:T(8,128)(2,1)}), bf16[256,4,256]{0,2,1:T(8,128)(2,1)S(1)}, u32[]{:S(2)}, u32[]{:S(2)}) %all-to-all-start.2) | async-done | bytes 524320 | tf_op jit(solution)/shard_map/all_to_all | solution.py:55
  37.0 3.5 all-to-all-start.3
  40.4 6.4 %copy.85 = bf16[256,8192]{0,1:T(8,128)(2,1)} copy(bf16[256,8192]{1,0:T(8,128)(2,1)} %param.16) | data formatting | bytes 8388608 | tf_op jit(solution)/shard_map/all_to_all | solution.py:53
  46.9 7.4 %all-to-all-done.3 = bf16[256,4,256]{0,2,1:T(8,128)(2,1)S(1)} async-done(((bf16[256,4,256]{0,2,1:T(8,128)(2,1)}), bf16[256,4,256]{0,2,1:T(8,128)(2,1)S(1)}, u32[]{:S(2)}, u32[]{:S(2)}) %all-to-all-start.3) | async-done | bytes 524320 | tf_op jit(solution)/shard_map/all_to_all | solution.py:54
  54.3 5.0 %all-to-all-start = ((bf16[256,4,2048]{0,2,1:T(8,128)(2,1)}), bf16[256,4,2048]{0,2,1:T(8,128)(2,1)}, u32[]{:S(2)}, u32[]{:S(2)}) async-start(bf16[256,4,2048]{0,2,1:T(8,128)(2,1)} %bitcast.214), calls=%async_computation | async-start | bytes 8388608 | tf_op jit(solution)/shard_map/all_to_all | solution.py:53
  59.7 92.3 %all-to-all-done = bf16[256,4,2048]{0,2,1:T(8,128)(2,1)} async-done(((bf16[256,4,2048]{0,2,1:T(8,128)(2,1)}), bf16[256,4,2048]{0,2,1:T(8,128)(2,1)}, u32[]{:S(2)}, u32[]{:S(2)}) %all-to-all-start) | async-done | bytes 4194336 | tf_op jit(solution)/shard_map/all_to_all | solution.py:53
  152.0 65.0 %while.45 = (s32[]{:T(128)}, f32[4,256,32,64]{1,3,2,0:T(8,128)}, f32[4,32,64,128]{3,2,1,0:T(8,128)}, f32[4,32]{1,0:T(4,128)S(1)}, f32[4,256,32]{1,2,0:T(8,128)S(...) while((s32[]{:T(128)}, f32[4,256,32,64]{1,3,2,0:T(8,128)}, ...), condition=%wide.region_3.4_spmd, body=%wide.region_0.3_spmd.sunk | while | flops 451789952 | bytes 20424928 | solution.py:71
  160.1 4.0 bitcast_dynamic-update-slice_fusion.4
  176.4 3.9 bitcast_dynamic-update-slice_fusion.4
  180.9 2.7 fusion.64
  192.6 3.9 bitcast_dynamic-update-slice_fusion.4
  208.9 3.9 bitcast_dynamic-update-slice_fusion.4
  217.0 5.8 %while.47 = (s32[]{:T(128)}, f32[32]{0:T(128)S(1)}, f32[32,64,128]{2,1,0:T(8,128)S(1)}, f32[4,32]{1,0:T(4,128)S(1)}, f32[4,32,64,128]{3,2,1,0:T(8,128)}, /*index=5*/s32[]{:T(128)}, s32[]{:T(128)}) while((s32[]{:T(128)}, f32[32]{0:T(128)S(1)}, f32[32,64,128]{2,1,0:T(8,128)S(1)}, f32[4,32]{1,0:T(4,128)S(1)}, ...), condition=%wide.region_5.6_spmd.clone, body=%wide.region_4.5_spmd.clone.sunk | while | flops 786499 | bytes 3146464 | solution.py:81
  225.5 13.4 %all-reduce = f32[256]{0:T(256)S(1)} all-reduce(f32[256]{0:T(256)S(1)} %dynamic-update-slice), channel_id=2, replica_groups=mesh['ctx'=8,'head'=4] {'ctx'}, use_global_device_ids=true, to_apply=%add | all-reduce | flops 256 | bytes 2048
  239.1 38.3 %all-gather.4.cloned.1.call-done = f32[256,64,128]{2,1,0:T(8,128)} async-done(((f32[32,64,128]{2,1,0:T(8,128)}), f32[256,64,128]{2,1,0:T(8,128)}) %all-gather.4.cloned.1.call-update) | async-done | bytes 8388624 | tf_op jit(solution)/shard_map/all_gather | solution.py:92
  277.5 4.1 multiply_reduce_fusion.1
  281.6 22.9 %while.46 = (s32[]{:T(128)}, f32[32,64,128]{2,1,0:T(8,128)S(1)}, bf16[4,256,32,64]{1,3,2,0:T(8,128)(2,1)}, f32[4,32]{1,0:T(4,128)S(1)}, f32[4,32,64,128]{3,2,1,0...) while((s32[]{:T(128)}, f32[32,64,128]{2,1,0:T(8,128)S(1)}, ...), condition=%wide.region_9.10_spmd, body=%wide.region_8.9_spmd.sunk | while | flops 138158080 | bytes 13076361 | solution.py:113
  282.1 3.7 fusion.68
  287.8 3.7 fusion.68
  293.5 3.7 fusion.68
  299.3 3.7 fusion.68
  304.4 6.3 %copy.81 = bf16[4,256,2048]{2,1,0:T(8,128)(2,1)} copy(bf16[4,256,2048]{1,2,0:T(8,128)(2,1)} %bitcast.218) | data formatting | bytes 8388608 | tf_op jit(solution)/shard_map/all_to_all | solution.py:117
  310.7 4.8 %all-to-all-start.4 = ((bf16[4,256,2048]{2,1,0:T(8,128)(2,1)}), bf16[4,256,2048]{2,1,0:T(8,128)(2,1)}, u32[]{:S(2)}, u32[]{:S(2)}) async-start(bf16[4,256,2048]{2,1,0:T(8,128)(2,1)} %copy.81), calls=%async_computation.4 | async-start | bytes 8388608 | tf_op jit(solution)/shard_map/all_to_all | solution.py:117
  315.5 6.4 %copy.83 = bf16[256,8192]{0,1:T(8,128)(2,1)} copy(bf16[256,8192]{1,0:T(8,128)(2,1)} %param.17) | data formatting | bytes 8388608 | tf_op args[1]
  321.9 87.5 %all-to-all-done.4 = bf16[4,256,2048]{2,1,0:T(8,128)(2,1)} async-done(((bf16[4,256,2048]{2,1,0:T(8,128)(2,1)}), bf16[4,256,2048]{2,1,0:T(8,128)(2,1)}, u32[]{:S(2)}, u32[]{:S(2)}) %all-to-all-start.4) | async-done | bytes 4194336 | tf_op jit(solution)/shard_map/all_to_all | solution.py:117
  409.4 6.2 %copy.82 = bf16[4,256,2048]{1,2,0:T(8,128)(2,1)} copy(bf16[4,256,2048]{2,1,0:T(8,128)(2,1)} %all-to-all-done.4) | data formatting | bytes 8388608 | tf_op jit(solution)/shard_map/all_to_all | solution.py:117
  415.7 5.3 %multiply_reduce_fusion = f32[256]{0:T(256)S(1)} fusion(bf16[256,8192]{0,1:T(8,128)(2,1)} %copy.83, bf16[4,256,2048]{1,2,0:T(8,128)(2,1)} %copy.82), kind=kLoop, calls=%fused_computation.70 | loop fusion | flops 18874112 | bytes 8389632 | tf_op jit(solution)/shard_map/reduce_sum | solution.py:119
  421.6 4.3 multiply_convert_fusion.2
  425.8 6.3 %copy.84 = bf16[256,8192]{1,0:T(8,128)(2,1)} copy(bf16[256,8192]{0,1:T(8,128)(2,1)} %multiply_convert_fusion.2) | data formatting | bytes 8388608 | tf_op jit(solution)/shard_map/convert_element_type | solution.py:120
  (169 shorter events, 65.8 us)
Async XLA Ops:
  8.1 12.1 %all-to-all-start.1 = ((bf16[256,4,32]{0,2,1:T(8,128)(2,1)}), bf16[256,4,32]{0,2,1:T(8,128)(2,1)S(1)}, u32[]{:S(2)}, u32[]{:S(2)}) async-start(bf16[256,4,32]{0,2,1:T(8,128)(2,1)} %bitcast.29), calls=%async_computation.1 | async-start | bytes 131072 | tf_op jit(solution)/shard_map/all_to_all | solution.py:56
  20.2 16.8 %all-to-all-start.2 = ((bf16[256,4,256]{0,2,1:T(8,128)(2,1)}), bf16[256,4,256]{0,2,1:T(8,128)(2,1)S(1)}, u32[]{:S(2)}, u32[]{:S(2)}) async-start(bf16[256,4,256]{0,2,1:T(8,128)(2,1)} %bitcast.31), calls=%async_computation.2 | async-start | bytes 1048576 | tf_op jit(solution)/shard_map/all_to_all | solution.py:55
  37.0 17.3 %all-to-all-start.3 = ((bf16[256,4,256]{0,2,1:T(8,128)(2,1)}), bf16[256,4,256]{0,2,1:T(8,128)(2,1)S(1)}, u32[]{:S(2)}, u32[]{:S(2)}) async-start(bf16[256,4,256]{0,2,1:T(8,128)(2,1)} %bitcast.34), calls=%async_computation.3 | async-start | bytes 1048576 | tf_op jit(solution)/shard_map/all_to_all | solution.py:54
  54.3 5.1 %copy-start.6 = (f32[32]{0:T(128)S(1)}, f32[32]{0:T(128)}, u32[]{:S(2)}) copy-start(f32[32]{0:T(128)} %param.22) | copy-start | bytes 388
  54.3 97.7 %copy-start.3 = (f32[32]{0:T(128)S(1)}, f32[32]{0:T(128)}, u32[]{:S(2)}) copy-start(f32[32]{0:T(128)} %param.21) | copy-start | bytes 388
  54.3 97.7 %copy-start.7 = (s32[4]{0:T(128)S(1)}, s32[4]{0:T(128)}, u32[]{:S(2)}) copy-start(s32[4]{0:T(128)} %param.25) | copy-start | bytes 52
  54.3 97.7 %all-to-all-start = ((bf16[256,4,2048]{0,2,1:T(8,128)(2,1)}), bf16[256,4,2048]{0,2,1:T(8,128)(2,1)}, u32[]{:S(2)}, u32[]{:S(2)}) async-start(bf16[256,4,2048]{0,2,1:T(8,128)(2,1)} %bitcast.214), calls=%async_computation | async-start | bytes 8388608 | tf_op jit(solution)/shard_map/all_to_all | solution.py:53
  59.3 218.2 %all-gather.4.cloned.1.call-start = ((), (), s32[]{:S(2)}) async-start(), calls=%async_computation.5 | async-start | bytes 9437184 | tf_op jit(solution)/shard_map/all_gather | solution.py:92
  217.0 6.9 %copy-start.8 = (u32[32]{0:T(128)S(1)}, u32[32]{0:T(128)}, u32[]{:S(2)}) copy-start(u32[32]{0:T(128)} %constant.102) | copy-start | bytes 388
  222.8 1.1 copy-start.2
  277.5 4.1 copy-start.5
  310.7 98.7 %all-to-all-start.4 = ((bf16[4,256,2048]{2,1,0:T(8,128)(2,1)}), bf16[4,256,2048]{2,1,0:T(8,128)(2,1)}, u32[]{:S(2)}, u32[]{:S(2)}) async-start(bf16[4,256,2048]{2,1,0:T(8,128)(2,1)} %copy.81), calls=%async_computation.4 | async-start | bytes 8388608 | tf_op jit(solution)/shard_map/all_to_all | solution.py:117
  409.4 11.5 %copy-start.4 = (f32[8192]{0:T(1024)S(1)}, f32[8192]{0:T(1024)}, u32[]{:S(2)}) copy-start(f32[8192]{0:T(1024)} %param.24) | copy-start | bytes 98308
  415.7 5.3 %copy-start = (bf16[256,8192]{0,1:T(8,128)(2,1)S(1)}, bf16[256,8192]{0,1:T(8,128)(2,1)}, u32[]{:S(2)}) copy-start(bf16[256,8192]{0,1:T(8,128)(2,1)} %copy.83) | copy-start | bytes 12582916
  415.7 5.9 %copy-start.1 = (bf16[4,256,2048]{1,2,0:T(8,128)(2,1)S(1)}, bf16[4,256,2048]{1,2,0:T(8,128)(2,1)}, u32[]{:S(2)}) copy-start(bf16[4,256,2048]{1,2,0:T(8,128)(2,1)} %copy.82) | copy-start | bytes 12582916
Sparse Core Ops, SparseCore 0:
  224.0 53.3 all-gather.3
where the time goes:
time: 441 us; the launch traced here: 439 us
  waiting for transfers between devices  241 us (55%)
  other arithmetic  51.1 us (12%)
  local copies, waits for them, and re-layouts  50.9 us (12%)
  matrix products  42.1 us (10%)
  starting transfers between devices  23.1 us (5%)
  between operations  14.3 us (3%)
  blocking collectives  13.4 us (3%)
    all_to_all x1, waiting for transfers between devices, local(): lax.all_to_all(head_inputs, 'head', split_axis=1, concat_axis=0, tiled=True)  92.3 us
    all_to_all x1, waiting for transfers between devices, local(): lax.all_to_all(scanned, 'head', split_axis=0, concat_axis=1, tiled=True)  87.5 us
    all_gather x1, waiting for transfers between devices, local(): lax.all_gather(own_state[None], 'ctx', axis=0, tiled=True)  38.3 us
    dot_general x4, matrix products, block_terms(): jnp.einsum('hts,shp->thp', mixing, block_x, preferred_element_type=jnp.fl...  15.8 us
    dot_general x4, matrix products, advance(): jnp.einsum('thn,hpn->thp', query_heads, frozen, preferred_element_type=jn...  14.8 us
    unnamed x25, local copies, waits for them, and re-layouts  14.5 us
    unnamed x1, blocking collectives  13.4 us
    all_to_all x2, local copies, waits for them, and re-layouts, local(): lax.all_to_all(scanned, 'head', split_axis=0, concat_axis=1, tiled=True)  12.5 us
  transfers between devices with their start and end apart: 6, of which 6 were waited for; matrix products, arithmetic and copies ran while one was open for 4% of the time, Pallas kernels for 0%

commit v1 on v0

v1 whole, which is shorter than its diff:
```python
import functools

import jax
import jax.numpy as jnp
from jax import lax
from jax.experimental import pallas as pl
from jax.experimental.pallas import tpu as pltpu
from jax.sharding import PartitionSpec as P

HEAD_DIM = 64
STATE = 128
BLOCK = 256
CHUNK = 512
SKEW = 2
MESH = pl.DeviceIdType.MESH
F32 = jnp.float32
BF16 = jnp.bfloat16


def split_terms(value, terms):
    parts = []
    for _ in range(terms):
        part = value.astype(BF16)
        parts.append(part)
        value = value - part.astype(F32)
    return parts


def spread_matrix(heads, first_head, width):
    row = lax.broadcasted_iota(jnp.int32, (2 * heads, width), 0)
    lane = lax.broadcasted_iota(jnp.int32, (2 * heads, width), 1)
    own = lane // HEAD_DIM + first_head
    return jnp.where((row == own) | (row == own + heads), 1.0, 0.0).astype(BF16)


def exchange_kernel(
    n, m, groups,
    x_ref, b_ref, logit_ref, param_ref, start_ref,
    frozen_ref, up_ref, down_ref, rows_ref,
    tail_ref, coef_ref, wide_ref, own_ref, sum_ref, before_ref,
    step_send, step_recv, fore_send, fore_recv, back_send, back_recv,
    param_in, decay_out, decay_in, hop_out, hop_in,
    param_sems, decay_sems, hop_sems, step_sems, fore_sems, back_sems,
):
    ci = lax.axis_index("ctx")
    zi = lax.axis_index("head")
    bits = m.bit_length() - 1
    length, inner = x_ref.shape
    heads = logit_ref.shape[1]
    count = inner // CHUNK
    per_group = count // groups

    def ctx_partner(j):
        bit = 1 << j
        upper = lax.rem(ci // bit, 2)
        return ci + bit - 2 * bit * upper, upper

    barrier = pltpu.get_barrier_semaphore()
    for d in range(1, n):
        pl.semaphore_signal(barrier, inc=1, device_id=(ci, lax.rem(zi + d, n)), device_id_type=MESH)
    for j in range(bits):
        pl.semaphore_signal(barrier, inc=1, device_id=(ctx_partner(j)[0], zi), device_id_type=MESH)
    pl.semaphore_wait(barrier, n - 1 + bits)

    def remote(src, dst, sems, index, device):
        return pltpu.make_async_remote_copy(
            src_ref=src, dst_ref=dst, send_sem=sems.at[(0, *index)], recv_sem=sems.at[(1, *index)],
            device_id=device, device_id_type=MESH,
        )

    def peer(d):
        return (ci, lax.rem(zi + d, n))

    param_copies = [
        remote(param_ref, param_in.at[d], param_sems, (d,), peer(d)) for d in range(1, n)
    ]
    for copy in param_copies:
        copy.start()
    for copy in param_copies:
        copy.wait()
    params = param_ref[...]
    for d in range(1, n):
        params = params + param_in[d]

    logits = logit_ref[...].astype(F32) + params[0:1]
    step = jnp.maximum(logits, 0.0) + jnp.log1p(jnp.exp(-jnp.abs(logits)))
    rate = -jnp.exp(params[1:2]) * step
    row = lax.broadcasted_iota(jnp.int32, (length, length), 0)
    col = lax.broadcasted_iota(jnp.int32, (length, length), 1)
    lower = jnp.where(row >= col, 1.0, 0.0).astype(BF16)
    cum = jnp.zeros((length, heads), F32)
    for part in split_terms(rate, 3)[::-1]:
        cum = cum + jnp.dot(lower, part, preferred_element_type=F32)
    last = cum[length - 1 : length]
    middle = cum[length // 2 - 1 : length // 2]
    start = start_ref[0:1, 0:1]
    position = lax.broadcasted_iota(jnp.int32, (length, heads), 0)
    begins = start < length
    keep = position >= jnp.where(begins, start, 0)
    tail = jnp.where(keep, jnp.exp(last - cum), 0.0) * step
    carried = jnp.where(begins, 0.0, jnp.exp(last))
    tail_ref[...] = jnp.concatenate(split_terms(tail, 2), axis=1)
    up_ref[...] = jnp.concatenate(split_terms(jnp.exp(cum - middle), 2), axis=1)
    down_ref[...] = jnp.concatenate(split_terms(jnp.exp(middle - cum) * step, 2), axis=1)

    decay_out[...] = jnp.broadcast_to(carried, decay_out.shape)
    decay_copies = [
        remote(decay_out, decay_in.at[d], decay_sems, (d,), peer(d)) for d in range(1, n)
    ]
    for copy in decay_copies:
        copy.start()
    for copy in decay_copies:
        copy.wait()
    before = jnp.ones((8, heads), F32)
    after = jnp.ones((8, heads), F32)
    for d in range(1, n):
        got = decay_in[d]
        before = before * jnp.where(zi >= d, got, 1.0)
        after = after * jnp.where(zi >= d, 1.0, got)
    own = jnp.broadcast_to(carried, (8, heads))
    total = before * own * after
    ahead = jnp.ones((8, heads), F32)
    coefs = [jnp.exp(jnp.broadcast_to(middle, (8, heads))), jnp.broadcast_to(params[2:3], (8, heads)), own, before, after]
    for j in range(bits):
        partner, upper = ctx_partner(j)
        hop_out[j] = total
        copy = remote(hop_out.at[j], hop_in.at[j], hop_sems, (j,), (partner, zi))
        copy.start()
        copy.wait()
        got = hop_in[j]
        is_upper = upper == 1
        coefs.append(jnp.where(is_upper, 1.0, got))
        coefs.append(jnp.where(is_upper, total, 1.0))
        coefs.append(jnp.where(is_upper, ahead, 0.0))
        ahead = jnp.where(is_upper, ahead * got, ahead)
        total = total * got
    slots = coef_ref.shape[0]
    pad = [jnp.zeros((1, heads), F32)] * (slots - len(coefs))
    table = jnp.concatenate([c[0:1] for c in coefs] + pad, axis=0)
    parts = split_terms(table, 3)
    first = jnp.concatenate(parts[:2], axis=1)

    def widen(k, _):
        matrix = spread_matrix(heads, k * (CHUNK // HEAD_DIM), CHUNK)
        wide = jnp.dot(first, matrix, preferred_element_type=F32)
        wide_ref[k] = wide
        rows_ref[k] = wide[0:8]
        return 0

    lax.fori_loop(0, count, widen, 0)

    fore_at = (bits + zi) * SKEW
    back_at = (bits + n - 1 - zi) * SKEW
    done_at = jnp.maximum(fore_at, back_at)

    def step_copy(j, k):
        return remote(step_send.at[j, k], step_recv.at[j, k], step_sems, (j, k), (ctx_partner(j)[0], zi))

    def fore_copy(k):
        return remote(fore_send.at[k], fore_recv.at[k], fore_sems, (k,), (ci, lax.rem(zi + 1, n)))

    def back_copy(k):
        return remote(back_send.at[k], back_recv.at[k], back_sems, (k,), (ci, lax.rem(zi + n - 1, n)))

    def line(k, slot):
        return wide_ref[k, slot : slot + 1, :]

    def iteration(t, _):
        @pl.when(t < count)
        def _():
            k = t
            matrix = spread_matrix(heads, k * (CHUNK // HEAD_DIM), CHUNK)
            weight = jnp.dot(tail_ref[...], matrix, preferred_element_type=F32)
            channels = pl.ds(pl.multiple_of(k * CHUNK, CHUNK), CHUNK)
            scaled = (x_ref[:, channels].astype(F32) * weight).astype(BF16)
            keys = b_ref[:, pl.ds(pl.multiple_of((k // per_group) * STATE, STATE), STATE)]
            written = lax.dot_general(keys, scaled, (((0,), (0,)), ((), ())), preferred_element_type=F32)
            own_ref[k] = written
            value = written * line(k, 4)
            sum_ref[k] = value
            before_ref[k] = jnp.zeros_like(value)
            step_send[0, k] = value.astype(BF16)
            step_copy(0, k).start()

        for j in range(bits):
            k = t - (j + 1) * SKEW

            @pl.when((k >= 0) & (k < count))
            def _(j=j, k=k):
                step_copy(j, k).wait_recv()
                got = step_recv[j, k].astype(F32)
                before_ref[k] += line(k, 7 + 3 * j) * got
                if j < bits - 1:
                    value = sum_ref[k] * line(k, 5 + 3 * j) + line(k, 6 + 3 * j) * got
                    sum_ref[k] = value
                    step_send[j + 1, k] = value.astype(BF16)
                    step_copy(j + 1, k).start()

        kf = t - fore_at

        @pl.when((kf >= 0) & (kf < count))
        def _():
            @pl.when(zi > 0)
            def _():
                fore_copy(kf).wait_recv()

            @pl.when(zi == 0)
            def _():
                fore_recv[kf] = jnp.zeros_like(fore_recv[kf])

            @pl.when(zi < n - 1)
            def _():
                arrived = fore_recv[kf].astype(F32) + line(kf, 3) * before_ref[kf]
                fore_send[kf] = (line(kf, 2) * arrived + own_ref[kf]).astype(BF16)
                fore_copy(kf).start()

        kb = t - back_at

        @pl.when((kb >= 0) & (kb < count))
        def _():
            @pl.when(zi < n - 1)
            def _():
                back_copy(kb).wait_recv()

            @pl.when(zi == n - 1)
            def _():
                back_recv[kb] = jnp.zeros_like(back_recv[kb])

            @pl.when(zi > 0)
            def _():
                back_send[kb] = (back_recv[kb].astype(F32) + before_ref[kb]).astype(BF16)
                back_copy(kb).start()

        kd = t - done_at

        @pl.when((kd >= 0) & (kd < count))
        def _():
            incoming = before_ref[kd] + back_recv[kd].astype(F32)
            frozen_ref[kd] = (fore_recv[kd].astype(F32) + line(kd, 3) * incoming).astype(BF16)

        return 0

    lax.fori_loop(0, count + (bits + n - 1) * SKEW, iteration, 0)

    def drain(k, _):
        for j in range(bits):
            step_copy(j, k).wait_send()

        @pl.when(zi < n - 1)
        def _():
            fore_copy(k).wait_send()

        @pl.when(zi > 0)
        def _():
            back_copy(k).wait_send()

        return 0

    lax.fori_loop(0, count, drain, 0)


def mix_kernel(
    x_ref, gate_ref, b_ref, c_ref, frozen_ref, up_ref, down_ref, rows_ref, start_ref, gain_ref,
    out_ref, gated_ref, power_ref,
):
    g = pl.program_id(0)
    length, width = x_ref.shape
    heads = up_ref.shape[1] // 2
    per_group = width // CHUNK
    start = start_ref[0:1, 0:1]
    row = lax.broadcasted_iota(jnp.int32, (length, length), 0)
    col = lax.broadcasted_iota(jnp.int32, (length, length), 1)
    allowed = (row >= col) & ((row >= start) == (col >= start))
    queries = c_ref[...]
    scores = lax.dot_general(queries, b_ref[...], (((1,), (1,)), ((), ())), preferred_element_type=F32)
    scores = jnp.where(allowed, scores, 0.0).astype(BF16)
    position = lax.broadcasted_iota(jnp.int32, (length, CHUNK), 0)
    power = jnp.zeros((length, 1), F32)
    for i in range(per_group):
        channels = slice(i * CHUNK, (i + 1) * CHUNK)
        k = g * per_group + i
        matrix = spread_matrix(heads, k * (CHUNK // HEAD_DIM), CHUNK)
        up = jnp.dot(up_ref[...], matrix, preferred_element_type=F32)
        down = jnp.dot(down_ref[...], matrix, preferred_element_type=F32)
        x = x_ref[:, channels].astype(F32)
        inside = jnp.dot(scores, (x * down).astype(BF16), preferred_element_type=F32)
        outside = jnp.dot(queries, frozen_ref[i], preferred_element_type=F32)
        outside = jnp.where(position < start, outside * rows_ref[i, 0:1, :], 0.0)
        mixed = (up * (inside + outside) + rows_ref[i, 1:2, :] * x).astype(BF16).astype(F32)
        gate = gate_ref[:, channels].astype(F32)
        gated = mixed * (gate / (1.0 + jnp.exp(-gate)))
        gated_ref[k] = gated
        power = power + jnp.sum(gated * gated, axis=1, keepdims=True)
    power_ref[...] = jnp.where(g == 0, 0.0, power_ref[...]) + jnp.broadcast_to(power, power_ref.shape)

    @pl.when(g == pl.num_programs(0) - 1)
    def _():
        count = gated_ref.shape[0]
        factor = lax.rsqrt(power_ref[:, 0:1] / (count * CHUNK) + 1e-05)
        for k in range(count):
            channels = slice(k * CHUNK, (k + 1) * CHUNK)
            out_ref[:, channels] = (gated_ref[k] * factor * gain_ref[0:1, channels]).astype(BF16)


def local(
    n, m,
    head_inputs, gate_inputs, write_keys, read_queries, step_logits,
    step_bias, decay_log, skip_scale, norm_gain, document_starts,
):
    length, inner = head_inputs.shape
    heads = step_logits.shape[1]
    groups = write_keys.shape[1] // STATE
    assert length <= BLOCK and BLOCK % length == 0 and m & (m - 1) == 0
    bits = m.bit_length() - 1
    count = inner // CHUNK
    per_group = count // groups
    zi = lax.axis_index("head")
    own = step_bias.shape[0]
    params = jnp.stack([step_bias, decay_log, skip_scale])
    params = lax.dynamic_update_slice(jnp.zeros((8, heads), F32), params, (0, zi * own))
    offset = lax.rem(zi * length, BLOCK)
    start = lax.dynamic_index_in_dim(document_starts, zi * length // BLOCK, keepdims=False) - offset
    start = jnp.where((start < 0) | (start >= length), length, start)
    start = jnp.broadcast_to(start, (8, 128)).astype(jnp.int32)

    slots = 24
    assert 5 + 3 * bits <= slots
    vmem = pl.BlockSpec(memory_space=pltpu.VMEM)
    piece = (count, STATE, CHUNK)
    dma = pltpu.SemaphoreType.DMA
    frozen, up, down, rows = pl.pallas_call(
        functools.partial(exchange_kernel, n, m, groups),
        out_shape=(
            jax.ShapeDtypeStruct(piece, BF16),
            jax.ShapeDtypeStruct((length, 2 * heads), BF16),
            jax.ShapeDtypeStruct((length, 2 * heads), BF16),
            jax.ShapeDtypeStruct((count, 8, CHUNK), F32),
        ),
        in_specs=[vmem] * 5,
        out_specs=(vmem,) * 4,
        scratch_shapes=[
            pltpu.VMEM((length, 2 * heads), BF16),
            pltpu.VMEM((24, heads), F32),
            pltpu.VMEM((count, 24, CHUNK), F32),
            pltpu.VMEM(piece, F32),
            pltpu.VMEM(piece, F32),
            pltpu.VMEM(piece, F32),
            pltpu.VMEM((bits, *piece), BF16),
            pltpu.VMEM((bits, *piece), BF16),
            pltpu.VMEM(piece, BF16),
            pltpu.VMEM(piece, BF16),
            pltpu.VMEM(piece, BF16),
            pltpu.VMEM(piece, BF16),
            pltpu.VMEM((n, 8, heads), F32),
            pltpu.VMEM((8, heads), F32),
            pltpu.VMEM((n, 8, heads), F32),
            pltpu.VMEM((bits, 8, heads), F32),
            pltpu.VMEM((bits, 8, heads), F32),
            dma((2, n)),
            dma((2, n)),
            dma((2, bits)),
            dma((2, bits, count)),
            dma((2, count)),
            dma((2, count)),
        ],
        compiler_params=pltpu.CompilerParams(
            collective_id=0, has_side_effects=True, vmem_limit_bytes=60 * 2**20
        ),
        name="exchange",
    )(head_inputs, write_keys, step_logits, params, start)

    width = per_group * CHUNK
    whole = lambda g: (0, 0)
    return pl.pallas_call(
        mix_kernel,
        grid=(groups,),
        out_shape=jax.ShapeDtypeStruct((length, inner), BF16),
        in_specs=[
            pl.BlockSpec((length, width), lambda g: (0, g)),
            pl.BlockSpec((length, width), lambda g: (0, g)),
            pl.BlockSpec((length, STATE), lambda g: (0, g)),
            pl.BlockSpec((length, STATE), lambda g: (0, g)),
            pl.BlockSpec((per_group, STATE, CHUNK), lambda g: (g, 0, 0)),
            pl.BlockSpec((length, 2 * heads), whole),
            pl.BlockSpec((length, 2 * heads), whole),
            pl.BlockSpec((per_group, 8, CHUNK), lambda g: (g, 0, 0)),
            pl.BlockSpec((8, 128), whole),
            pl.BlockSpec((1, inner), whole),
        ],
        out_specs=pl.BlockSpec((length, inner), whole),
        scratch_shapes=[
            pltpu.VMEM((count, length, CHUNK), F32),
            pltpu.VMEM((length, 128), F32),
        ],
        compiler_params=pltpu.CompilerParams(vmem_limit_bytes=60 * 2**20),
        name="mix",
    )(head_inputs, gate_inputs, write_keys, read_queries, frozen, up, down, rows, start, norm_gain[None])


def solution(mesh):
    tokens = P(("ctx", "head"), None)
    return jax.shard_map(
        functools.partial(local, mesh.shape["head"], mesh.shape["ctx"]),
        mesh=mesh,
        in_specs=(tokens,) * 5 + (P("head"), P("head"), P("head"), P(), P("ctx")),
        out_specs=tokens,
        check_vma=False,
    )
```

time: 441 us -> 120 us (0.27)
  waiting for transfers between devices: 241 us -> 0 us
  Pallas kernels: 0 us -> 116 us
  other arithmetic: 51.1 us -> 0.7 us
  local copies, waits for them, and re-layouts: 50.9 us -> 2.62 us
  matrix products: 42.1 us -> 0 us
  starting transfers between devices: 23.1 us -> 0 us
  between operations: 14.3 us -> 0.69 us
  blocking collectives: 13.4 us -> 0 us
    all_to_all x5 -> x0, waiting for transfers between devices: 202 us -> none  [the longest x1 92.3 us: local(): lax.all_to_all(head_inputs, 'head', split_axis=1, concat_axis=0, tiled=True)]
    pallas_call x0 -> x2, Pallas kernels: none -> 116 us  [the longest x1 98.5 us: local(): pl.pallas_call(functools.partial(exchange_kernel, n, m, groups), out_shap...]
    dot_general x16 -> x0, matrix products: 42.1 us -> none  [the longest x4 15.8 us: block_terms(): jnp.einsum('hts,shp->thp', mixing, block_x, preferred_element_type=jnp.fl...]
    all_gather x1 -> x0, waiting for transfers between devices: 38.3 us -> none  [local(): lax.all_gather(own_state[None], 'ctx', axis=0, tiled=True)]
    all_to_all x5 -> x0, starting transfers between devices: 23.1 us -> none  [the longest x1 6.35 us: local(): lax.all_to_all(step_logits, 'head', split_axis=1, concat_axis=0, tiled=True)]
    all_to_all x3 -> x0, local copies, waits for them, and re-layouts: 18.9 us -> none  [the longest x2 12.5 us: local(): lax.all_to_all(scanned, 'head', split_axis=0, concat_axis=1, tiled=True)]
    convert_element_type x5 -> x0, other arithmetic: 14.4 us -> none  [the longest x4 10.1 us: block_terms(): mixing = (damping * scores * step_size.T[:, None, :]).astype(jnp.bfloat16)]
    unnamed x25 -> x2, local copies, waits for them, and re-layouts: 14.5 us -> 0.59 us
  transfers between devices with their start and end apart: 6 -> 0, of which waited for: 6 -> 0; matrix products, arithmetic and copies ran while one was open for 4% -> 0% of each run, Pallas kernels for 0% -> 0%
where the time goes in v1:
time: 120 us
  Pallas kernels  116 us (97%)
  local copies, waits for them, and re-layouts  2.62 us (2%)
    pallas_call x1, Pallas kernels, local(): pl.pallas_call(functools.partial(exchange_kernel, n, m, groups), out_shap...  98.5 us
    pallas_call x1, Pallas kernels, local(): pl.pallas_call(mix_kernel, grid=(groups,), out_shape=jax.ShapeDtypeStruct...  17.7 us

profile of v1, /device:TPU:0, one launch (start us, length us, event | category | flops | bytes accessed | tf_op | source)
XLA Modules:
  0.0 120.2 jit_solution(1027076848221482930)
XLA Ops:
  0.0 1.2 %dynamic_slice.4 = s32[1]{0:T(128)} dynamic-slice(s32[4]{0:T(128)} %param.19, s32[]{:T(128)S(6)} %select_n.18), dynamic_slice_sizes={1} | dynamic-slice | bytes 12 | tf_op jit(solution)/shard_map/jit(dynamic_index_in_dim)/dynamic_slice | solution.py:322
  1.9 0.7 pad_maximum_fusion
  2.6 0.6 broadcast_in_dim.10.start_ref
  3.2 0.2 dynamic_update_slice.3.param_ref
  3.4 0.0 copy-start
  3.4 0.6 copy-done
  4.0 98.5 %exchange.1 = (bf16[16,128,512]{2,1,0:T(8,128)(2,1)}, bf16[256,256]{1,0:T(8,128)(2,1)}, bf16[256,256]{1,0:T(8,128)(2,1)}, f32[16,8,512]{2,1,0:T(8,128)}) custom-call(bf16[256,8192]{1,0:T(8,128)(2,1)} %x_ref.3, bf16[256,1024]{1,0:T(8,128)(2,1)} %b_ref.3, bf16[256,128]{1,0:T(8,128)(2,1)} %logit_ref.1, f32[8,128]{1,0:T(8,128)} %copy-done, ...), custom_call_target="tpu_custom_call" | custom-call | tf_op jit(solution)/shard_map/exchange/pallas_call | solution.py:331
  102.5 17.7 %mix.1 = bf16[256,8192]{1,0:T(8,128)(2,1)} custom-call(bf16[256,8192]{1,0:T(8,128)(2,1)} %x_ref.3, bf16[256,8192]{1,0:T(8,128)(2,1)} %gate_ref.1, bf16[256,1024]{1,0:T(8,128)(2,1)} %b_ref.3, bf16[256,1024]{1,0:T(8,128)(2,1)} %c_ref.1, bf16[16,128,512]{2,1,0:T(8,128)(2,1)} %get-tuple-element.9.frozen_ref, bf16[256,256]{1,0:T(8,128)(2,1)} %get-tuple-element.10.up_ref, ...), custom_call_target="tpu_custom_call" | custom-call | tf_op jit(solution)/shard_map/mix/pallas_call | solution.py:374
  (1 shorter events, 0.0 us)
Async XLA Ops:
  3.4 0.6 copy-start

commit v2 on v1

v2 whole, which is shorter than its diff:
```python
import functools

import jax
import jax.numpy as jnp
from jax import lax
from jax.experimental import pallas as pl
from jax.experimental.pallas import tpu as pltpu
from jax.sharding import PartitionSpec as P

HEAD_DIM = 64
STATE = 128
BLOCK = 256
CHUNK = 256
SKEW = 2
ROWS = 32
MESH = pl.DeviceIdType.MESH
F32 = jnp.float32
BF16 = jnp.bfloat16


def split_terms(value, terms):
    parts = []
    for _ in range(terms):
        part = value.astype(BF16)
        parts.append(part)
        value = value - part.astype(F32)
    return parts


def spread_matrix(heads, first_head, width):
    row = lax.broadcasted_iota(jnp.int32, (2 * heads, width), 0)
    lane = lax.broadcasted_iota(jnp.int32, (2 * heads, width), 1)
    own = lane // HEAD_DIM + first_head
    return jnp.where((row == own) | (row == own + heads), 1.0, 0.0).astype(BF16)


def exchange_kernel(
    n, m, groups,
    x_hbm, b_ref, c_ref, logit_ref, bias_ref, decay_ref, skip_ref, starts_ref,
    mixed_hbm,
    x_ref, scores_ref, mixed_ref, param_ref,
    tail_ref, up_ref, down_ref, wide_ref, own_ref, sum_ref, before_ref,
    step_send, step_recv, fore_send, fore_recv, back_send, back_recv,
    param_in, decay_out, decay_in, hop_out, hop_in,
    param_sems, decay_sems, hop_sems, step_sems, fore_sems, back_sems, x_sem, mixed_sems,
):
    ci = lax.axis_index("ctx")
    zi = lax.axis_index("head")
    bits = m.bit_length() - 1
    length, inner = x_ref.shape
    heads = logit_ref.shape[1]
    count = inner // CHUNK
    per_group = count // groups
    chunk_heads = CHUNK // HEAD_DIM

    load_x = pltpu.make_async_copy(x_hbm, x_ref, x_sem)
    load_x.start()

    def ctx_partner(j):
        bit = 1 << j
        upper = lax.rem(ci // bit, 2)
        return ci + bit - 2 * bit * upper, upper

    barrier = pltpu.get_barrier_semaphore()
    for d in range(1, n):
        pl.semaphore_signal(barrier, inc=1, device_id=(ci, lax.rem(zi + d, n)), device_id_type=MESH)
    for j in range(bits):
        pl.semaphore_signal(barrier, inc=1, device_id=(ctx_partner(j)[0], zi), device_id_type=MESH)

    own_heads = bias_ref.shape[1]
    place = jnp.where(
        lax.broadcasted_iota(jnp.int32, (own_heads, heads), 0) + zi * own_heads
        == lax.broadcasted_iota(jnp.int32, (own_heads, heads), 1), 1.0, 0.0
    ).astype(BF16)
    raw = jnp.concatenate(
        [bias_ref[...], decay_ref[...], skip_ref[...], jnp.zeros((5, own_heads), F32)], axis=0
    )
    placed = jnp.zeros((8, heads), F32)
    for part in split_terms(raw, 3):
        placed = placed + jnp.dot(part, place, preferred_element_type=F32)
    param_ref[...] = placed
    pl.semaphore_wait(barrier, n - 1 + bits)

    def remote(src, dst, sems, index, device):
        return pltpu.make_async_remote_copy(
            src_ref=src, dst_ref=dst, send_sem=sems.at[(0, *index)], recv_sem=sems.at[(1, *index)],
            device_id=device, device_id_type=MESH,
        )

    def peer(d):
        return (ci, lax.rem(zi + d, n))

    param_copies = [
        remote(param_ref, param_in.at[d], param_sems, (d,), peer(d)) for d in range(1, n)
    ]
    for copy in param_copies:
        copy.start()

    offset = lax.rem(zi * length, BLOCK)
    starts = starts_ref[...].astype(F32)
    mine = lax.broadcasted_iota(jnp.int32, starts.shape, 1) == zi * length // BLOCK
    start = jnp.sum(jnp.where(mine, starts, 0.0), axis=1, keepdims=True) - offset.astype(F32)
    start = jnp.where((start < 0.0) | (start >= length), float(length), start)
    row = lax.broadcasted_iota(jnp.int32, (length, length), 0).astype(F32)
    col = lax.broadcasted_iota(jnp.int32, (length, length), 1).astype(F32)
    lower = jnp.where(row >= col, 1.0, 0.0)
    same = jnp.where(row >= start, 1.0, 0.0) == jnp.where(col >= start, 1.0, 0.0)
    allowed = jnp.where(same, lower, 0.0)
    for g in range(groups):
        part = slice(g * STATE, (g + 1) * STATE)
        scores = lax.dot_general(
            c_ref[:, part], b_ref[:, part], (((1,), (1,)), ((), ())), preferred_element_type=F32
        )
        scores_ref[g] = jnp.where(allowed > 0.0, scores, 0.0).astype(BF16)

    for copy in param_copies:
        copy.wait()
    params = param_ref[...]
    for d in range(1, n):
        params = params + param_in[d]

    logits = logit_ref[...].astype(F32) + params[0:1]
    step = jnp.maximum(logits, 0.0) + jnp.log1p(jnp.exp(-jnp.abs(logits)))
    rate = -jnp.exp(params[1:2]) * step
    lower = lower.astype(BF16)
    cum = jnp.zeros((length, heads), F32)
    for part in split_terms(rate, 3)[::-1]:
        cum = cum + jnp.dot(lower, part, preferred_element_type=F32)
    last = cum[length - 1 : length]
    middle = cum[length // 2 - 1 : length // 2]
    position = lax.broadcasted_iota(jnp.int32, (length, heads), 0).astype(F32)
    begins = start < length
    carried = jnp.where(begins, 0.0, jnp.exp(last))

    decay_out[...] = jnp.broadcast_to(carried, decay_out.shape)
    decay_copies = [
        remote(decay_out, decay_in.at[d], decay_sems, (d,), peer(d)) for d in range(1, n)
    ]
    for copy in decay_copies:
        copy.start()
    keep = position >= jnp.where(begins, start, 0.0)
    tail = jnp.where(keep, jnp.exp(last - cum), 0.0) * step
    tail_ref[...] = jnp.concatenate(split_terms(tail, 2), axis=1)
    up_ref[...] = jnp.concatenate(split_terms(jnp.exp(cum - middle), 2), axis=1)
    down_ref[...] = jnp.concatenate(split_terms(jnp.exp(middle - cum) * step, 2), axis=1)
    load_x.wait()
    for copy in decay_copies:
        copy.wait()
    before = jnp.ones((8, heads), F32)
    after = jnp.ones((8, heads), F32)
    for d in range(1, n):
        got = decay_in[d]
        before = before * jnp.where(zi >= d, got, 1.0)
        after = after * jnp.where(zi >= d, 1.0, got)
    own = jnp.broadcast_to(carried, (8, heads))
    total = before * own * after
    ahead = jnp.ones((8, heads), F32)
    after_parts = jnp.concatenate(split_terms(after, 2), axis=1)

    def step_copy(j, k):
        return remote(step_send.at[j, k], step_recv.at[j, k], step_sems, (j, k), (ctx_partner(j)[0], zi))

    def fore_copy(k):
        return remote(fore_send.at[k], fore_recv.at[k], fore_sems, (k,), (ci, lax.rem(zi + 1, n)))

    def back_copy(k):
        return remote(back_send.at[k], back_recv.at[k], back_sems, (k,), (ci, lax.rem(zi + n - 1, n)))

    def store_copy(k):
        channels = pl.ds(pl.multiple_of(k * CHUNK, CHUNK), CHUNK)
        return pltpu.make_async_copy(mixed_ref.at[k], mixed_hbm.at[:, channels], mixed_sems.at[k])

    def line(k, slot):
        return wide_ref[k, slot : slot + 1, :]

    is_last_upper = ctx_partner(bits - 1)[1] == 1
    is_last_lower = ctx_partner(bits - 1)[1] == 0

    def write(k, _):
        matrix = spread_matrix(heads, k * chunk_heads, CHUNK)
        weight = jnp.dot(tail_ref[...], matrix, preferred_element_type=F32)
        scale = jnp.dot(after_parts, matrix, preferred_element_type=F32)[0:1]
        channels = pl.ds(pl.multiple_of(k * CHUNK, CHUNK), CHUNK)
        scaled = (x_ref[:, channels].astype(F32) * weight).astype(BF16)
        keys = b_ref[:, pl.ds(pl.multiple_of((k // per_group) * STATE, STATE), STATE)]
        written = lax.dot_general(keys, scaled, (((0,), (0,)), ((), ())), preferred_element_type=F32)
        own_ref[k] = written
        value = written * scale
        sum_ref[k] = value
        step_send[0, k] = value.astype(BF16)
        step_copy(0, k).start()
        return 0

    middle_factor = jnp.broadcast_to(jnp.exp(middle), (8, heads))
    coefs = [middle_factor, jnp.broadcast_to(params[2:3], (8, heads)), own, before]
    for j in range(bits + 1):
        if j < bits:
            partner, upper = ctx_partner(j)
            hop_out[j] = total
            copy = remote(hop_out.at[j], hop_in.at[j], hop_sems, (j,), (partner, zi))
            copy.start()
        lax.fori_loop(j * count // (bits + 1), (j + 1) * count // (bits + 1), write, 0)
        if j < bits:
            copy.wait()
            got = hop_in[j]
            is_upper = upper == 1
            coefs.append(jnp.where(is_upper, 1.0, got))
            coefs.append(jnp.where(is_upper, total, 1.0))
            coefs.append(jnp.where(is_upper, ahead, 0.0))
            ahead = jnp.where(is_upper, ahead * got, ahead)
            total = total * got
    slots = wide_ref.shape[1]
    pad = [jnp.zeros((1, heads), F32)] * (slots - len(coefs))
    table = jnp.concatenate([c[0:1] for c in coefs] + pad, axis=0)
    table = jnp.concatenate(split_terms(table, 2), axis=1)

    fore_at = (bits - 1 + zi) * SKEW
    back_at = (bits - 1 + n - 1 - zi) * SKEW
    done_at = jnp.maximum(fore_at, back_at)

    def iteration(t, _):
        for j in range(bits):
            k = t - j * SKEW

            @pl.when((k >= 0) & (k < count))
            def _(j=j, k=k):
                if j == 0:
                    matrix = spread_matrix(heads, k * chunk_heads, CHUNK)
                    wide_ref[k] = jnp.dot(table, matrix, preferred_element_type=F32)
                    before_ref[k] = jnp.zeros_like(before_ref[k])

                def receive():
                    step_copy(j, k).wait_recv()
                    got = step_recv[j, k].astype(F32)
                    before_ref[k] += line(k, 6 + 3 * j) * got
                    return got

                if j == bits - 1:
                    @pl.when(is_last_upper)
                    def _():
                        receive()

                else:
                    got = receive()
                    value = sum_ref[k] * line(k, 4 + 3 * j) + line(k, 5 + 3 * j) * got
                    sum_ref[k] = value

                    def send():
                        step_send[j + 1, k] = value.astype(BF16)
                        step_copy(j + 1, k).start()

                    if j == bits - 2:
                        pl.when(is_last_lower)(send)
                    else:
                        send()

        kf = t - fore_at

        @pl.when((kf >= 0) & (kf < count))
        def _():
            @pl.when(zi > 0)
            def _():
                fore_copy(kf).wait_recv()

            @pl.when(zi == 0)
            def _():
                fore_recv[kf] = jnp.zeros_like(fore_recv[kf])

            @pl.when(zi < n - 1)
            def _():
                arrived = fore_recv[kf].astype(F32) + line(kf, 3) * before_ref[kf]
                fore_send[kf] = (line(kf, 2) * arrived + own_ref[kf]).astype(BF16)
                fore_copy(kf).start()

        kb = t - back_at

        @pl.when((kb >= 0) & (kb < count))
        def _():
            @pl.when(zi < n - 1)
            def _():
                back_copy(kb).wait_recv()

            @pl.when(zi == n - 1)
            def _():
                back_recv[kb] = jnp.zeros_like(back_recv[kb])

            @pl.when(zi > 0)
            def _():
                back_send[kb] = (back_recv[kb].astype(F32) + before_ref[kb]).astype(BF16)
                back_copy(kb).start()

        kd = t - done_at

        @pl.when((kd >= 0) & (kd < count))
        def _():
            incoming = before_ref[kd] + back_recv[kd].astype(F32)
            frozen = (fore_recv[kd].astype(F32) + line(kd, 3) * incoming).astype(BF16)
            matrix = spread_matrix(heads, kd * chunk_heads, CHUNK)
            up = jnp.dot(up_ref[...], matrix, preferred_element_type=F32)
            down = jnp.dot(down_ref[...], matrix, preferred_element_type=F32)
            x = x_ref[:, pl.ds(pl.multiple_of(kd * CHUNK, CHUNK), CHUNK)].astype(F32)
            group = kd // per_group
            inside = jnp.dot(scores_ref[group], (x * down).astype(BF16), preferred_element_type=F32)
            queries = c_ref[:, pl.ds(pl.multiple_of(group * STATE, STATE), STATE)]
            outside = jnp.dot(queries, frozen, preferred_element_type=F32)
            place_in = lax.broadcasted_iota(jnp.int32, outside.shape, 0).astype(F32)
            outside = jnp.where(place_in < start, outside * line(kd, 0), 0.0)
            mixed_ref[kd] = (up * (inside + outside) + line(kd, 1) * x).astype(BF16)
            store_copy(kd).start()

        return 0

    lax.fori_loop(0, count + (bits - 1 + n - 1) * SKEW, iteration, 0)

    def drain(k, _):
        for j in range(bits - 1):
            step_copy(j, k).wait_send()

        @pl.when(is_last_lower)
        def _():
            step_copy(bits - 1, k).wait_send()

        @pl.when(zi < n - 1)
        def _():
            fore_copy(k).wait_send()

        @pl.when(zi > 0)
        def _():
            back_copy(k).wait_send()

        store_copy(k).wait()
        return 0

    lax.fori_loop(0, count, drain, 0)


def norm_kernel(mixed_ref, gate_ref, gain_ref, out_ref, gated_ref):
    rows, inner = mixed_ref.shape
    width = 1024
    power = jnp.zeros((rows, 1), F32)
    for i in range(inner // width):
        channels = slice(i * width, (i + 1) * width)
        gate = gate_ref[:, channels].astype(F32)
        gated = mixed_ref[:, channels].astype(F32) * (gate / (1.0 + jnp.exp(-gate)))
        gated_ref[:, channels] = gated
        power = power + jnp.sum(gated * gated, axis=1, keepdims=True)
    factor = lax.rsqrt(power / inner + 1e-05)
    for i in range(inner // width):
        channels = slice(i * width, (i + 1) * width)
        out_ref[:, channels] = (gated_ref[:, channels] * factor * gain_ref[:, channels]).astype(BF16)


def local(
    n, m,
    head_inputs, gate_inputs, write_keys, read_queries, step_logits,
    step_bias, decay_log, skip_scale, norm_gain, document_starts,
):
    length, inner = head_inputs.shape
    heads = step_logits.shape[1]
    groups = write_keys.shape[1] // STATE
    assert length <= BLOCK and BLOCK % length == 0 and m & (m - 1) == 0 and m > 1
    bits = m.bit_length() - 1
    count = inner // CHUNK

    slots = 24
    assert 4 + 3 * bits <= slots
    vmem = pl.BlockSpec(memory_space=pltpu.VMEM)
    hbm = pl.BlockSpec(memory_space=pl.ANY)
    piece = (count, STATE, CHUNK)
    dma = pltpu.SemaphoreType.DMA
    mixed = pl.pallas_call(
        functools.partial(exchange_kernel, n, m, groups),
        out_shape=jax.ShapeDtypeStruct((length, inner), BF16),
        in_specs=[hbm] + [vmem] * 7,
        out_specs=hbm,
        scratch_shapes=[
            pltpu.VMEM((length, inner), BF16),
            pltpu.VMEM((groups, length, length), BF16),
            pltpu.VMEM((count, length, CHUNK), BF16),
            pltpu.VMEM((8, heads), F32),
            pltpu.VMEM((length, 2 * heads), BF16),
            pltpu.VMEM((length, 2 * heads), BF16),
            pltpu.VMEM((length, 2 * heads), BF16),
            pltpu.VMEM((count, slots, CHUNK), F32),
            pltpu.VMEM(piece, F32),
            pltpu.VMEM(piece, F32),
            pltpu.VMEM(piece, F32),
            pltpu.VMEM((bits, *piece), BF16),
            pltpu.VMEM((bits, *piece), BF16),
            pltpu.VMEM(piece, BF16),
            pltpu.VMEM(piece, BF16),
            pltpu.VMEM(piece, BF16),
            pltpu.VMEM(piece, BF16),
            pltpu.VMEM((n, 8, heads), F32),
            pltpu.VMEM((8, heads), F32),
            pltpu.VMEM((n, 8, heads), F32),
            pltpu.VMEM((bits, 8, heads), F32),
            pltpu.VMEM((bits, 8, heads), F32),
            dma((2, n)),
            dma((2, n)),
            dma((2, bits)),
            dma((2, bits, count)),
            dma((2, count)),
            dma((2, count)),
            dma,
            dma((count,)),
        ],
        compiler_params=pltpu.CompilerParams(
            collective_id=0, has_side_effects=True, vmem_limit_bytes=60 * 2**20
        ),
        name="exchange",
    )(
        head_inputs, write_keys, read_queries, step_logits,
        step_bias[None], decay_log[None], skip_scale[None], document_starts[None],
    )

    tile = min(length, ROWS)
    tokens = pl.BlockSpec((tile, inner), lambda i: (i, 0))
    return pl.pallas_call(
        norm_kernel,
        grid=(length // tile,),
        out_shape=jax.ShapeDtypeStruct((length, inner), BF16),
        in_specs=[tokens, tokens, pl.BlockSpec((1, inner), lambda i: (0, 0))],
        out_specs=tokens,
        scratch_shapes=[pltpu.VMEM((tile, inner), F32)],
        compiler_params=pltpu.CompilerParams(vmem_limit_bytes=32 * 2**20),
        name="norm",
    )(mixed, gate_inputs, norm_gain[None])


def solution(mesh):
    tokens = P(("ctx", "head"), None)
    return jax.shard_map(
        functools.partial(local, mesh.shape["head"], mesh.shape["ctx"]),
        mesh=mesh,
        in_specs=(tokens,) * 5 + (P("head"), P("head"), P("head"), P(), P("ctx")),
        out_specs=tokens,
        check_vma=False,
    )
```

time: 120 us -> 112 us (0.933)
  Pallas kernels: 116 us -> 108 us
  local copies, waits for them, and re-layouts: 2.62 us -> 4.37 us
    pallas_call x1, Pallas kernels: 17.7 us -> 6.34 us  [local(): pl.pallas_call(norm_kernel, grid=(length // tile,), out_shape=jax.ShapeDt...]
    unnamed x2 -> x6, local copies, waits for them, and re-layouts: 0.59 us -> 4.37 us
    pallas_call x1, Pallas kernels: 98.5 us -> 101 us  [local(): pl.pallas_call(functools.partial(exchange_kernel, n, m, groups), out_shap...]
    dynamic_slice x1 -> x0, local copies, waits for them, and re-layouts: 1.24 us -> none  [local(): lax.dynamic_index_in_dim(document_starts, zi * length // BLOCK, keepdims=...]
where the time goes in v2:
time: 112 us
  Pallas kernels  108 us (96%)
  local copies, waits for them, and re-layouts  4.37 us (4%)
    pallas_call x1, Pallas kernels, local(): pl.pallas_call(functools.partial(exchange_kernel, n, m, groups), out_shap...  101 us
    pallas_call x1, Pallas kernels, local(): pl.pallas_call(norm_kernel, grid=(length // tile,), out_shape=jax.ShapeDt...  6.34 us
    unnamed x6, local copies, waits for them, and re-layouts  4.37 us

profile of v2, /device:TPU:0, one launch (start us, length us, event | category | flops | bytes accessed | tf_op | source)
XLA Modules:
  0.0 111.9 jit_solution(11961656458078050641)
XLA Ops:
  0.0 0.0 copy-start.2
  0.0 101.2 %exchange.1.mixed_ref = bf16[256,8192]{1,0:T(8,128)(2,1)} custom-call(bf16[256,8192]{1,0:T(8,128)(2,1)} %x_hbm.1, bf16[256,1024]{1,0:T(8,128)(2,1)} %b_ref.1, bf16[256,1024]{1,0:T(8,128)(2,1)} %c_ref.1, bf16[256,128]{1,0:T(8,128)(2,1)} %logit_ref.1, f32[1,32]{1,0:T(1,128)} %bitcast.6, f32[1,32]{1,0:T(1,128)} %bitcast.7, f32[1,32]{1,0:T(1,128)} %bitcast.8, ...), custom_call_target="tpu_custom_call" | custom-call | tf_op jit(solution)/shard_map/exchange/pallas_call | solution.py:371
  101.2 0.0 copy-done.2
  101.2 0.0 copy-start
  101.2 2.2 %copy-done = bf16[256,8192]{1,0:T(8,128)(2,1)S(1)} copy-done((bf16[256,8192]{1,0:T(8,128)(2,1)S(1)}, bf16[256,8192]{1,0:T(8,128)(2,1)}, u32[]{:S(2)}) %copy-start) | copy-done | bytes 4194328
  103.4 0.0 copy-start.1
  103.4 2.2 %copy-done.1 = bf16[256,8192]{1,0:T(8,128)(2,1)S(1)} copy-done((bf16[256,8192]{1,0:T(8,128)(2,1)S(1)}, bf16[256,8192]{1,0:T(8,128)(2,1)}, u32[]{:S(2)}) %copy-start.1) | copy-done | bytes 4194328
  105.6 6.3 %norm.1 = bf16[256,8192]{1,0:T(8,128)(2,1)} custom-call(bf16[256,8192]{1,0:T(8,128)(2,1)S(1)} %copy-done, bf16[256,8192]{1,0:T(8,128)(2,1)S(1)} %copy-done.1, f32[1,8192]{1,0:T(1,128)S(1)} %bitcast.5), custom_call_target="tpu_custom_call" | custom-call | tf_op jit(solution)/shard_map/norm/pallas_call | solution.py:419
Async XLA Ops:
  0.0 101.2 %copy-start.2 = (f32[8192]{0:T(1024)S(1)}, f32[8192]{0:T(1024)}, u32[]{:S(2)}) copy-start(f32[8192]{0:T(1024)} %param.18) | copy-start | bytes 98308
  101.2 2.2 %copy-start = (bf16[256,8192]{1,0:T(8,128)(2,1)S(1)}, bf16[256,8192]{1,0:T(8,128)(2,1)}, u32[]{:S(2)}) copy-start(bf16[256,8192]{1,0:T(8,128)(2,1)} %exchange.1.mixed_ref) | copy-start | bytes 12582916
  103.4 2.2 %copy-start.1 = (bf16[256,8192]{1,0:T(8,128)(2,1)S(1)}, bf16[256,8192]{1,0:T(8,128)(2,1)}, u32[]{:S(2)}) copy-start(bf16[256,8192]{1,0:T(8,128)(2,1)} %gate_ref.1) | copy-start | bytes 12582916

commit v3 on v2

--- a/solution.py
+++ b/solution.py
@@ -11,7 +11,8 @@
 STATE = 128
 BLOCK = 256
 CHUNK = 256
-SKEW = 2
+SKEW = 3
+EARLY = 2
 ROWS = 32
 MESH = pl.DeviceIdType.MESH
 F32 = jnp.float32
@@ -193,22 +194,20 @@
 
     middle_factor = jnp.broadcast_to(jnp.exp(middle), (8, heads))
     coefs = [middle_factor, jnp.broadcast_to(params[2:3], (8, heads)), own, before]
-    for j in range(bits + 1):
-        if j < bits:
-            partner, upper = ctx_partner(j)
-            hop_out[j] = total
-            copy = remote(hop_out.at[j], hop_in.at[j], hop_sems, (j,), (partner, zi))
-            copy.start()
-        lax.fori_loop(j * count // (bits + 1), (j + 1) * count // (bits + 1), write, 0)
-        if j < bits:
-            copy.wait()
-            got = hop_in[j]
-            is_upper = upper == 1
-            coefs.append(jnp.where(is_upper, 1.0, got))
-            coefs.append(jnp.where(is_upper, total, 1.0))
-            coefs.append(jnp.where(is_upper, ahead, 0.0))
-            ahead = jnp.where(is_upper, ahead * got, ahead)
-            total = total * got
+    for j in range(bits):
+        partner, upper = ctx_partner(j)
+        hop_out[j] = total
+        copy = remote(hop_out.at[j], hop_in.at[j], hop_sems, (j,), (partner, zi))
+        copy.start()
+        lax.fori_loop(j * EARLY, (j + 1) * EARLY, write, 0)
+        copy.wait()
+        got = hop_in[j]
+        is_upper = upper == 1
+        coefs.append(jnp.where(is_upper, 1.0, got))
+        coefs.append(jnp.where(is_upper, total, 1.0))
+        coefs.append(jnp.where(is_upper, ahead, 0.0))
+        ahead = jnp.where(is_upper, ahead * got, ahead)
+        total = total * got
     slots = wide_ref.shape[1]
     pad = [jnp.zeros((1, heads), F32)] * (slots - len(coefs))
     table = jnp.concatenate([c[0:1] for c in coefs] + pad, axis=0)
@@ -219,6 +218,12 @@
     done_at = jnp.maximum(fore_at, back_at)
 
     def iteration(t, _):
+        kw = t + bits * EARLY
+
+        @pl.when(kw < count)
+        def _():
+            write(kw, 0)
+
         for j in range(bits):
             k = t - j * SKEW
 
@@ -363,7 +368,7 @@
     count = inner // CHUNK
 
     slots = 24
-    assert 4 + 3 * bits <= slots
+    assert bits * EARLY <= count and 4 + 3 * bits <= slots
     vmem = pl.BlockSpec(memory_space=pltpu.VMEM)
     hbm = pl.BlockSpec(memory_space=pl.ANY)
     piece = (count, STATE, CHUNK)
@@ -406,7 +411,7 @@
             dma((count,)),
         ],
         compiler_params=pltpu.CompilerParams(
-            collective_id=0, has_side_effects=True, vmem_limit_bytes=60 * 2**20
+            collective_id=0, has_side_effects=True, vmem_limit_bytes=48 * 2**20
         ),
         name="exchange",
     )(
@@ -423,7 +428,7 @@
         in_specs=[tokens, tokens, pl.BlockSpec((1, inner), lambda i: (0, 0))],
         out_specs=tokens,
         scratch_shapes=[pltpu.VMEM((tile, inner), F32)],
-        compiler_params=pltpu.CompilerParams(vmem_limit_bytes=32 * 2**20),
+        compiler_params=pltpu.CompilerParams(vmem_limit_bytes=20 * 2**20),
         name="norm",
     )(mixed, gate_inputs, norm_gain[None])
 

time: 112 us -> 97.4 us (0.87)
  Pallas kernels: 108 us -> 91.6 us
  local copies, waits for them, and re-layouts: 4.37 us -> 5.55 us
    pallas_call x1, Pallas kernels: 101 us -> 85.2 us  [local(): pl.pallas_call(functools.partial(exchange_kernel, n, m, groups), out_shap...]
    unnamed x6 -> x18, local copies, waits for them, and re-layouts: 4.37 us -> 5.55 us
where the time goes in v3:
time: 97.4 us; the launch traced here: 97.2 us
  Pallas kernels  91.6 us (94%)
  local copies, waits for them, and re-layouts  5.55 us (6%)
    pallas_call x1, Pallas kernels, local(): pl.pallas_call(functools.partial(exchange_kernel, n, m, groups), out_shap...  85.2 us
    pallas_call x1, Pallas kernels, local(): pl.pallas_call(norm_kernel, grid=(length // tile,), out_shape=jax.ShapeDt...  6.36 us
    unnamed x18, local copies, waits for them, and re-layouts  5.55 us

profile of v3, /device:TPU:0, one launch (start us, length us, event | category | flops | bytes accessed | tf_op | source)
XLA Modules:
  0.0 97.2 jit_solution(5371018530140086056)
XLA Ops:
  0.0 0.0 copy-start.1
  0.0 1.0 %copy-done.1 = bf16[256,1024]{1,0:T(8,128)(2,1)S(1)} copy-done((bf16[256,1024]{1,0:T(8,128)(2,1)S(1)}, bf16[256,1024]{1,0:T(8,128)(2,1)}, u32[]{:S(2)}) %copy-start.1) | copy-done | bytes 524312
  1.0 0.0 copy-start.2
  1.0 1.0 %copy-done.2 = bf16[256,1024]{1,0:T(8,128)(2,1)S(1)} copy-done((bf16[256,1024]{1,0:T(8,128)(2,1)S(1)}, bf16[256,1024]{1,0:T(8,128)(2,1)}, u32[]{:S(2)}) %copy-start.2) | copy-done | bytes 524312
  2.1 0.0 copy-start.3
  2.1 0.8 copy-done.3
  2.9 0.0 copy-start.5
  2.9 0.7 copy-done.5
  3.6 0.0 copy-start.6
  3.6 0.7 copy-done.6
  4.2 0.0 copy-start.7
  4.2 0.7 copy-done.7
  4.9 0.0 copy-start.8
  4.9 0.7 copy-done.8
  5.5 0.0 copy-start
  5.5 0.0 copy-start.4
  5.6 85.2 %exchange.1.mixed_ref = bf16[256,8192]{1,0:T(8,128)(2,1)S(1)} custom-call(bf16[256,8192]{1,0:T(8,128)(2,1)} %x_hbm.1, bf16[256,1024]{1,0:T(8,128)(2,1)S(1)} %copy-done.1, bf16[256,1024]{1,0:T(8,128)(2,1)S(1)} %copy-done.2, bf16[256,128]{1,0:T(8,128)(2,1)S(1)} %copy-done.3, f32[1,32]{1,0:T(1,128)S(1)} %bitcast.6, f32[1,32]{1,0:T(1,128)S(1)} %bitcast.7, ...), custom_call_target="tpu_custom_call" | custom-call | tf_op jit(solution)/shard_map/exchange/pallas_call | solution.py:376
  90.8 0.0 copy-done
  90.8 0.0 copy-done.4
  90.8 6.4 %norm.1 = bf16[256,8192]{1,0:T(8,128)(2,1)} custom-call(bf16[256,8192]{1,0:T(8,128)(2,1)S(1)} %exchange.1.mixed_ref, bf16[256,8192]{1,0:T(8,128)(2,1)S(1)} %copy-done, f32[1,8192]{1,0:T(1,128)S(1)} %bitcast.5), custom_call_target="tpu_custom_call" | custom-call | tf_op jit(solution)/shard_map/norm/pallas_call | solution.py:424
Async XLA Ops:
  0.0 1.0 %copy-start.1 = (bf16[256,1024]{1,0:T(8,128)(2,1)S(1)}, bf16[256,1024]{1,0:T(8,128)(2,1)}, u32[]{:S(2)}) copy-start(bf16[256,1024]{1,0:T(8,128)(2,1)} %b_ref.1) | copy-start | bytes 1572868
  1.0 1.0 %copy-start.2 = (bf16[256,1024]{1,0:T(8,128)(2,1)S(1)}, bf16[256,1024]{1,0:T(8,128)(2,1)}, u32[]{:S(2)}) copy-start(bf16[256,1024]{1,0:T(8,128)(2,1)} %c_ref.1) | copy-start | bytes 1572868
  2.1 0.8 copy-start.3
  2.9 0.7 copy-start.5
  3.6 0.7 copy-start.6
  4.2 0.7 copy-start.7
  4.9 0.7 copy-start.8
  5.5 85.2 %copy-start = (bf16[256,8192]{1,0:T(8,128)(2,1)S(1)}, bf16[256,8192]{1,0:T(8,128)(2,1)}, u32[]{:S(2)}) copy-start(bf16[256,8192]{1,0:T(8,128)(2,1)} %gate_ref.1) | copy-start | bytes 12582916
  5.5 85.2 %copy-start.4 = (f32[8192]{0:T(1024)S(1)}, f32[8192]{0:T(1024)}, u32[]{:S(2)}) copy-start(f32[8192]{0:T(1024)} %param.18) | copy-start | bytes 98308

commit v4 on v3

--- a/solution.py
+++ b/solution.py
@@ -37,13 +37,13 @@
 
 def exchange_kernel(
     n, m, groups,
-    x_hbm, b_ref, c_ref, logit_ref, bias_ref, decay_ref, skip_ref, starts_ref,
+    x_hbm, b_hbm, c_hbm, logit_hbm, bias_hbm, decay_hbm, skip_hbm, starts_hbm,
     mixed_hbm,
-    x_ref, scores_ref, mixed_ref, param_ref,
+    x_ref, b_ref, c_ref, logit_ref, bias_ref, decay_ref, skip_ref, starts_ref, scores_ref, mixed_ref, param_ref,
     tail_ref, up_ref, down_ref, wide_ref, own_ref, sum_ref, before_ref,
     step_send, step_recv, fore_send, fore_recv, back_send, back_recv,
     param_in, decay_out, decay_in, hop_out, hop_in,
-    param_sems, decay_sems, hop_sems, step_sems, fore_sems, back_sems, x_sem, mixed_sems,
+    param_sems, decay_sems, hop_sems, step_sems, fore_sems, back_sems, load_sems, mixed_sems,
 ):
     ci = lax.axis_index("ctx")
     zi = lax.axis_index("head")
@@ -54,8 +54,13 @@
     per_group = count // groups
     chunk_heads = CHUNK // HEAD_DIM
 
-    load_x = pltpu.make_async_copy(x_hbm, x_ref, x_sem)
-    load_x.start()
+    pairs = (
+        (bias_hbm, bias_ref), (decay_hbm, decay_ref), (skip_hbm, skip_ref), (starts_hbm, starts_ref),
+        (b_hbm, b_ref), (c_hbm, c_ref), (logit_hbm, logit_ref), (x_hbm, x_ref),
+    )
+    loads = [pltpu.make_async_copy(src, dst, load_sems.at[i]) for i, (src, dst) in enumerate(pairs)]
+    for load in loads:
+        load.start()
 
     def ctx_partner(j):
         bit = 1 << j
@@ -73,6 +78,8 @@
         lax.broadcasted_iota(jnp.int32, (own_heads, heads), 0) + zi * own_heads
         == lax.broadcasted_iota(jnp.int32, (own_heads, heads), 1), 1.0, 0.0
     ).astype(BF16)
+    for load in loads[:4]:
+        load.wait()
     raw = jnp.concatenate(
         [bias_ref[...], decay_ref[...], skip_ref[...], jnp.zeros((5, own_heads), F32)], axis=0
     )
@@ -107,6 +114,8 @@
     lower = jnp.where(row >= col, 1.0, 0.0)
     same = jnp.where(row >= start, 1.0, 0.0) == jnp.where(col >= start, 1.0, 0.0)
     allowed = jnp.where(same, lower, 0.0)
+    for load in loads[4:7]:
+        load.wait()
     for g in range(groups):
         part = slice(g * STATE, (g + 1) * STATE)
         scores = lax.dot_general(
@@ -144,7 +153,7 @@
     tail_ref[...] = jnp.concatenate(split_terms(tail, 2), axis=1)
     up_ref[...] = jnp.concatenate(split_terms(jnp.exp(cum - middle), 2), axis=1)
     down_ref[...] = jnp.concatenate(split_terms(jnp.exp(middle - cum) * step, 2), axis=1)
-    load_x.wait()
+    loads[7].wait()
     for copy in decay_copies:
         copy.wait()
     before = jnp.ones((8, heads), F32)
@@ -369,17 +378,24 @@
 
     slots = 24
     assert bits * EARLY <= count and 4 + 3 * bits <= slots
-    vmem = pl.BlockSpec(memory_space=pltpu.VMEM)
-    hbm = pl.BlockSpec(memory_space=pl.ANY)
+    hbm = pl.BlockSpec(memory_space=pltpu.HBM)
+    anywhere = pl.BlockSpec(memory_space=pl.ANY)
     piece = (count, STATE, CHUNK)
     dma = pltpu.SemaphoreType.DMA
     mixed = pl.pallas_call(
         functools.partial(exchange_kernel, n, m, groups),
         out_shape=jax.ShapeDtypeStruct((length, inner), BF16),
-        in_specs=[hbm] + [vmem] * 7,
-        out_specs=hbm,
+        in_specs=[hbm] * 8,
+        out_specs=anywhere,
         scratch_shapes=[
             pltpu.VMEM((length, inner), BF16),
+            pltpu.VMEM(write_keys.shape, BF16),
+            pltpu.VMEM(read_queries.shape, BF16),
+            pltpu.VMEM(step_logits.shape, BF16),
+            pltpu.VMEM((1, step_bias.shape[0]), F32),
+            pltpu.VMEM((1, step_bias.shape[0]), F32),
+            pltpu.VMEM((1, step_bias.shape[0]), F32),
+            pltpu.VMEM((1, document_starts.shape[0]), jnp.int32),
             pltpu.VMEM((groups, length, length), BF16),
             pltpu.VMEM((count, length, CHUNK), BF16),
             pltpu.VMEM((8, heads), F32),
@@ -407,11 +423,11 @@
             dma((2, bits, count)),
             dma((2, count)),
             dma((2, count)),
-            dma,
+            dma((8,)),
             dma((count,)),
         ],
         compiler_params=pltpu.CompilerParams(
-            collective_id=0, has_side_effects=True, vmem_limit_bytes=48 * 2**20
+            collective_id=0, has_side_effects=True, vmem_limit_bytes=56 * 2**20
         ),
         name="exchange",
     )(

time: 97.4 us -> 94.3 us (0.968)
  local copies, waits for them, and re-layouts: 5.55 us -> 2.19 us
    unnamed x18 -> x6, local copies, waits for them, and re-layouts: 5.55 us -> 2.19 us
where the time goes in v4:
time: 94.3 us; the launch traced here: 94.2 us
  Pallas kernels  91.9 us (97%)
  local copies, waits for them, and re-layouts  2.19 us (2%)
    pallas_call x1, Pallas kernels, local(): pl.pallas_call(functools.partial(exchange_kernel, n, m, groups), out_shap...  85.6 us
    pallas_call x1, Pallas kernels, local(): pl.pallas_call(norm_kernel, grid=(length // tile,), out_shape=jax.ShapeDt...  6.34 us
    unnamed x6, local copies, waits for them, and re-layouts  2.19 us

profile of v4, /device:TPU:0, one launch (start us, length us, event | category | flops | bytes accessed | tf_op | source)
XLA Modules:
  0.0 94.2 jit_solution(9276936966697916038)
XLA Ops:
  0.0 0.0 copy-start.1
  0.0 0.0 copy-start.2
  0.0 85.6 %exchange.1.mixed_ref = bf16[256,8192]{1,0:T(8,128)(2,1)} custom-call(bf16[256,8192]{1,0:T(8,128)(2,1)} %x_hbm.1, bf16[256,1024]{1,0:T(8,128)(2,1)} %b_hbm.1, bf16[256,1024]{1,0:T(8,128)(2,1)} %c_hbm.1, bf16[256,128]{1,0:T(8,128)(2,1)} %logit_hbm.1, f32[1,32]{1,0:T(1,128)} %bitcast.6, f32[1,32]{1,0:T(1,128)} %bitcast.7, f32[1,32]{1,0:T(1,128)} %bitcast.8, ...), custom_call_target="tpu_custom_call" | custom-call | tf_op jit(solution)/shard_map/exchange/pallas_call | solution.py:385
  85.6 0.0 copy-done.1
  85.6 0.0 copy-done.2
  85.6 0.0 copy-start
  85.7 2.2 %copy-done = bf16[256,8192]{1,0:T(8,128)(2,1)S(1)} copy-done((bf16[256,8192]{1,0:T(8,128)(2,1)S(1)}, bf16[256,8192]{1,0:T(8,128)(2,1)}, u32[]{:S(2)}) %copy-start) | copy-done | bytes 4194328
  87.8 6.3 %norm.1 = bf16[256,8192]{1,0:T(8,128)(2,1)} custom-call(bf16[256,8192]{1,0:T(8,128)(2,1)S(1)} %copy-done, bf16[256,8192]{1,0:T(8,128)(2,1)S(1)} %copy-done.1, f32[1,8192]{1,0:T(1,128)S(1)} %bitcast.5), custom_call_target="tpu_custom_call" | custom-call | tf_op jit(solution)/shard_map/norm/pallas_call | solution.py:440
Async XLA Ops:
  0.0 85.6 %copy-start.1 = (bf16[256,8192]{1,0:T(8,128)(2,1)S(1)}, bf16[256,8192]{1,0:T(8,128)(2,1)}, u32[]{:S(2)}) copy-start(bf16[256,8192]{1,0:T(8,128)(2,1)} %gate_ref.1) | copy-start | bytes 12582916
  0.0 85.6 %copy-start.2 = (f32[8192]{0:T(1024)S(1)}, f32[8192]{0:T(1024)}, u32[]{:S(2)}) copy-start(f32[8192]{0:T(1024)} %param.18) | copy-start | bytes 98308
  85.6 2.2 %copy-start = (bf16[256,8192]{1,0:T(8,128)(2,1)S(1)}, bf16[256,8192]{1,0:T(8,128)(2,1)}, u32[]{:S(2)}) copy-start(bf16[256,8192]{1,0:T(8,128)(2,1)} %exchange.1.mixed_ref) | copy-start | bytes 12582916
